TPU v7x, 256 devices: a whole 4x4x8 slice. The times are simulated.
256 devices in a mesh: traj: 32 (over z, y), seg: 8 (over x, core).
Axes of the slice: x: 4, y: 4, z: 8, core: 2. Of those that a mesh axis runs over, the one named last changes fastest.
Arguments:
- coords: float32 [32, 1024, 3, 512], P('traj', 'seg')
- pairs: int32 [2, 1024], replicated, may hold values from 0 to 511, as said below
- lengths: int32 [32], P('traj'), may hold values from 1 to 1024, 24576 in all
Outputs:
- projected: float32 [32, 1024, 128], P('traj', 'seg')
Inputs may be any that keep to these rules, and one draw needn't show every extreme that they name: `pairs`: atom indices; the two atoms of a contact differ. `lengths`: each trajectory's recorded frames fill its first slots.
All inputs are finite; a program needn't handle non-finite values. No bound on the sum of `lengths` on one device may be relied on, other than what follows from the above.
Results may differ from a plain program's by a relative error of at most 0.0003.
Values sent between devices are 32-bit elements; how exact they have to be, the bound alone decides.
No kernel may reach another device: no remote copies, remote signals or barrier semaphores. Data moves between devices by JAX's collectives and lax.ppermute only.
A program may use at most 128 MiB of HBM per device.

v0:
```python
import jax
import jax.numpy as jnp
from jax import lax
from jax.sharding import PartitionSpec as P

K = 128
LAG = 10
ITERS = 3


exact_mode = lax.Precision.HIGHEST
soft_square = 0.1
ridge_term = 0.01
spectral_shift = 2.0


def from_behind(x, axis, by):
    peers = lax.axis_size(axis)
    pairs = [(i, i + by) for i in range(peers) if 0 <= i + by < peers]
    return lax.ppermute(x, axis, pairs)


def featurize(frames, pairs):
    first_atom = jnp.take(frames, pairs[0], axis=2)
    second_atom = jnp.take(frames, pairs[1], axis=2)
    offset = first_atom - second_atom
    return jnp.sqrt(jnp.sum(offset * offset, axis=1) + soft_square)


def tri_solve(factor, rhs, transposed):
    return lax.linalg.triangular_solve(
        factor, rhs, left_side=True, lower=True, transpose_a=transposed
    )


def cross_gram(left_rows, right_rows):
    return lax.dot_general(
        left_rows,
        right_rows,
        (((0,), (0,)), ((), ())),
        precision=exact_mode,
        preferred_element_type=jnp.float32,
    )


def row_sum(weights, matrix):
    return jnp.dot(weights, matrix, precision=exact_mode, preferred_element_type=jnp.float32)


def subspace(c_zero, c_lag, basis_width):
    lower_factor = jnp.linalg.cholesky(c_zero)
    identity = jnp.eye(c_zero.shape[0], dtype=jnp.float32)
    basis_q = identity[:, :basis_width]
    for sweep in range(ITERS):
        inner_solve = tri_solve(lower_factor, basis_q, True)
        moved_block = jnp.dot(
            c_lag, inner_solve, precision=exact_mode, preferred_element_type=jnp.float32
        )
        image_block = tri_solve(lower_factor, moved_block, False) + spectral_shift * basis_q
        gram_small = cross_gram(image_block, image_block)
        small_factor = jnp.linalg.cholesky(gram_small)
        basis_q = tri_solve(small_factor, image_block.T, False).T
    return tri_solve(lower_factor, basis_q, True)


def on_device(coords, pairs, lengths):
    frames = coords[0]
    frame_rows = frames.shape[0]
    features = featurize(frames, pairs)
    feature_count = features.shape[1]
    frame_index = lax.axis_index("seg") * frame_rows + jnp.arange(frame_rows, dtype=jnp.int32)
    length = lengths[0]
    is_valid = (frame_index < length).astype(jnp.float32)
    paired = (frame_index + LAG < length).astype(jnp.float32)
    arriving = from_behind(features[:LAG], "seg", -1)
    lagged = jnp.concatenate([features[LAG:], arriving], axis=0)
    count_all = jnp.sum(is_valid)
    count_pair = jnp.sum(paired)
    sum_all = row_sum(is_valid, features)
    sum_lead = row_sum(paired, features)
    sum_ahead = row_sum(paired, lagged)
    own_counts = jnp.stack([count_all, count_pair])[None, :]
    own_totals = jnp.stack([sum_all, sum_lead, sum_ahead])[None]
    all_counts, all_totals = (
        lax.all_gather(own_counts, ("traj", "seg"), axis=0, tiled=True),
        lax.all_gather(own_totals, ("traj", "seg"), axis=0, tiled=True),
    )
    frames_total = jnp.sum(all_counts[:, 0])
    pairs_total = jnp.sum(all_counts[:, 1])
    mean_all = jnp.sum(all_totals[:, 0], axis=0) / frames_total
    mean_lead = jnp.sum(all_totals[:, 1], axis=0) / pairs_total
    mean_ahead = jnp.sum(all_totals[:, 2], axis=0) / pairs_total
    center_all = sum_all / jnp.maximum(count_all, 1.0)
    center_lead = sum_lead / jnp.maximum(count_pair, 1.0)
    center_ahead = sum_ahead / jnp.maximum(count_pair, 1.0)
    centered = (features - center_all) * is_valid[:, None]
    lead_rows = (features - center_lead) * paired[:, None]
    ahead_rows = (lagged - center_ahead) * paired[:, None]
    gram_zero = cross_gram(centered, centered)
    gram_lag = cross_gram(lead_rows, ahead_rows)
    total_zero, total_lag = lax.psum((gram_zero, gram_lag), ("traj", "seg"))
    symmetric_lag = total_lag + total_lag.T
    safe_counts = jnp.maximum(all_counts, 1.0)
    spread_all = all_totals[:, 0] / safe_counts[:, 0:1] - mean_all
    spread_lead = all_totals[:, 1] / safe_counts[:, 1:2] - mean_lead
    spread_ahead = all_totals[:, 2] / safe_counts[:, 1:2] - mean_ahead
    total_zero = total_zero + cross_gram(spread_all * all_counts[:, 0:1], spread_all)
    between_lag = cross_gram(spread_lead * all_counts[:, 1:2], spread_ahead)
    symmetric_lag = symmetric_lag + between_lag + between_lag.T
    identity = jnp.eye(feature_count, dtype=jnp.float32)
    c_zero = total_zero / frames_total + ridge_term * identity
    c_lag = symmetric_lag / (2.0 * pairs_total)
    basis = subspace(c_zero, c_lag, K)
    shifted = (features - mean_all) * is_valid[:, None]
    projected = jnp.dot(shifted, basis, precision=exact_mode, preferred_element_type=jnp.float32)
    return projected[None]


def solution(mesh):
    return jax.shard_map(
        on_device,
        mesh=mesh,
        in_specs=(P("traj", "seg", None, None), P(), P("traj")),
        out_specs=P("traj", "seg", None),
        check_vma=False,
    )
```

profile of v0, /device:TPU:6, one launch (start us, length us, event | category | flops | bytes accessed | tf_op | source)
XLA Modules:
  0.0 1031.9 jit_solution(3482435308951660966)
XLA Ops:
  8.9 3.6 gather_fusion
  12.5 8.0 gather_fusion.1
  20.4 7.7 fusion.4
  34.7 5.6 fusion.27
  41.0 5.6 fusion.22
  48.8 79.8 %all-reduce.1 = f32[512]{0:T(512)S(1)} all-reduce(f32[512]{0:T(512)S(1)} %maximum_dynamic-update-slice_fusion), channel_id=3, replica_groups=mesh['traj'=32,'seg'=8] {'traj','seg'}, use_global_device_ids=true, to_apply=%add.1 | all-reduce | flops 512 | bytes 4096
  132.6 197.8 %all-reduce.5.cloned.1.call-done = (f32[1024,1024]{1,0:T(8,128)}, f32[1024,1024]{0,1:T(8,128)}) async-done(((f32[1024,1024]{1,0:T(8,128)}, f32[1024,1024]{0,1:T(8,128)}), (f32[1024,1024]{1,0:T(8,128)}, f32[1024,1024]{0,1:T(8,128)})) %all-reduce.5.cloned.1.call-update) | async-done | bytes 8388624 | tf_op jit(solution)/shard_map/psum | solution.py:101
  330.3 5.3 copy.134
  335.7 112.9 %all-gather.5.cloned.1.call-done = f32[256,3,1024]{2,1,0:T(4,128)} async-done(((f32[1,3,1024]{2,1,0:T(4,128)}), f32[256,3,1024]{2,1,0:T(4,128)}) %all-gather.5.cloned.1.call-update) | async-done | bytes 3145744 | tf_op jit(solution)/shard_map/all_gather | solution.py:86
  448.5 6.1 slice_reduce_fusion.2
  456.2 9.7 broadcast_multiply_fusion
  465.9 6.7 select_add_fusion
  472.5 5.7 copy.116
  478.3 4.4 fusion.2
  484.7 11.7 %cholesky.236 = f32[128,128]{1,0:T(8,128)S(1)} custom-call(f32[128,128]{1,0:T(8,128)S(1)} %cholesky.667), custom_call_target="Cholesky" | custom-call | tf_op jit(solution)/shard_map/jit(cholesky)/cholesky | solution.py:51
  496.5 9.8 custom-call.70
  510.2 11.7 %cholesky.259 = f32[128,128]{1,0:T(8,128)S(1)} custom-call(f32[128,128]{1,0:T(8,128)S(1)} %cholesky.671), custom_call_target="Cholesky" | custom-call | tf_op jit(solution)/shard_map/jit(cholesky)/cholesky | solution.py:51
  525.7 9.8 custom-call.71
  542.1 11.7 %cholesky.493 = f32[128,128]{1,0:T(8,128)S(1)} custom-call(f32[128,128]{1,0:T(8,128)S(1)} %cholesky.676), custom_call_target="Cholesky" | custom-call | tf_op jit(solution)/shard_map/jit(cholesky)/cholesky | solution.py:51
  554.6 9.8 custom-call.72
  565.6 3.3 convolution_subtract_fusion.2
  569.0 11.7 %cholesky.512 = f32[128,128]{1,0:T(8,128)S(1)} custom-call(f32[128,128]{1,0:T(8,128)S(1)} %cholesky.681), custom_call_target="Cholesky" | custom-call | tf_op jit(solution)/shard_map/jit(cholesky)/cholesky | solution.py:51
  581.5 9.8 custom-call.73
  592.4 3.1 convolution_subtract_fusion.3
  595.6 12.1 %cholesky.531 = f32[128,128]{1,0:T(8,128)S(1)} custom-call(f32[128,128]{1,0:T(8,128)S(1)} %cholesky.686), custom_call_target="Cholesky" | custom-call | tf_op jit(solution)/shard_map/jit(cholesky)/cholesky | solution.py:51
  608.5 9.8 custom-call.74
  619.4 3.1 convolution_subtract_fusion.4
  622.5 11.7 %cholesky.551 = f32[128,128]{1,0:T(8,128)S(1)} custom-call(f32[128,128]{1,0:T(8,128)S(1)} %cholesky.691), custom_call_target="Cholesky" | custom-call | tf_op jit(solution)/shard_map/jit(cholesky)/cholesky | solution.py:51
  635.0 9.8 custom-call.75
  645.8 2.8 convolution_subtract_fusion.5
  648.6 11.7 %cholesky.571 = f32[128,128]{1,0:T(8,128)S(1)} custom-call(f32[128,128]{1,0:T(8,128)S(1)} %cholesky.696), custom_call_target="Cholesky" | custom-call | tf_op jit(solution)/shard_map/jit(cholesky)/cholesky | solution.py:51
  661.1 9.8 custom-call.76
  674.0 11.7 %cholesky.589 = f32[128,128]{1,0:T(8,128)S(1)} custom-call(f32[128,128]{1,0:T(8,128)S(1)} %convolution_subtract_fusion.41), custom_call_target="Cholesky" | custom-call | tf_op jit(solution)/shard_map/jit(cholesky)/cholesky | solution.py:51
  696.5 4.9 select_select_fusion
  701.4 28.7 %while.14 = (s32[]{:T(128)}, f32[1024,1024]{0,1:T(8,128)}, s32[8,2]{0,1:T(2,128)S(1)}, f32[8,128,128]{2,1,0:T(8,128)}, s32[]{:T(128)}) while((s32[]{:T(128)}, f32[1024,1024]{0,1:T(8,128)}, s32[8,2]{0,1:T(2,128)S(1)}, f32[8,128,128]{2,1,0:T(8,128)}, s32[]{:T(128)}) %tuple.152), condition=%wide.while_cond.clone.2, body=%wide.while_body.clone.2.sunk | while | flops 2 | bytes 393829 | solution.py:31
  730.1 79.6 %custom-call.93 = f32[8,128,128]{1,2,0:T(8,128)S(1)} custom-call(f32[8,128,128]{2,1,0:T(8,128)} %get-tuple-element.62), custom_call_target="InvertDiagBlocksLowerTriangular" | custom-call | tf_op jit(solution)/shard_map/triangular_solve/custom-call.16 | solution.py:31
  824.7 5.2 fusion.6
  829.9 5.7 copy.135
  835.7 7.9 fusion
  845.5 3.4 fusion.333
  864.8 11.7 %cholesky.636 = f32[128,128]{1,0:T(8,128)S(1)} custom-call(f32[128,128]{1,0:T(8,128)S(1)} %fusion.231), custom_call_target="Cholesky" | custom-call | tf_op jit(solution)/shard_map/jit(cholesky)/cholesky | solution.py:61
  877.8 9.8 custom-call.86
  902.6 3.6 fusion.334
  922.3 12.1 %cholesky.647 = f32[128,128]{1,0:T(8,128)S(1)} custom-call(f32[128,128]{1,0:T(8,128)S(1)} %fusion.229), custom_call_target="Cholesky" | custom-call | tf_op jit(solution)/shard_map/jit(cholesky)/cholesky | solution.py:61
  935.8 9.8 custom-call.89
  959.7 3.6 fusion.335
  985.9 11.7 %cholesky.658 = f32[128,128]{1,0:T(8,128)S(1)} custom-call(f32[128,128]{1,0:T(8,128)S(1)} %fusion.227), custom_call_target="Cholesky" | custom-call | tf_op jit(solution)/shard_map/jit(cholesky)/cholesky | solution.py:61
  999.0 10.0 custom-call.92
  (409 shorter events, 195.6 us)
Async XLA Ops:
  6.5 323.8 %all-reduce.5.cloned.1.call-start = ((), (), s32[]{:S(2)}) async-start(), calls=%async_computation.1 | async-start | bytes 16777216 | tf_op jit(solution)/shard_map/psum | solution.py:101
  28.3 12.3 %collective-permute-start = (f32[10,1024]{0,1:T(8,128)S(1)}, f32[10,1024]{0,1:T(8,128)S(1)}, u32[]{:S(2)}, u32[]{:S(2)}) collective-permute-start(f32[10,1024]{0,1:T(8,128)S(1)} %bitcast.438), channel_id=1, source_target_pairs={{1,0},{2,1},{3,2},{4,3},{5,4},{6,5},{7,6},{9,8},{10,9},{11,10},{12... | collective-permute-start | bytes 122888 | tf_op jit(solution)/shard_map/ppermute | solution.py:20
  46.6 401.9 %all-gather.5.cloned.1.call-start = ((), (), s32[]{:S(2)}) async-start(), calls=%async_computation | async-start | bytes 4210688 | tf_op jit(solution)/shard_map/all_gather | solution.py:86
  130.7 1.0 copy-start.6
  454.6 11.3 %copy-start.11 = (f32[1024,1024]{0,1:T(8,128)S(1)}, f32[1024,1024]{0,1:T(8,128)}, u32[]{:S(2)}) copy-start(f32[1024,1024]{0,1:T(8,128)} %get-tuple-element.165) | copy-start | bytes 12582916
  482.7 2.0 copy-start.3
  509.4 0.8 copy-start.5
  523.0 12.5 %copy-start.4 = (f32[896,128]{0,1:T(8,128)S(1)}, f32[896,128]{0,1:T(8,128)}, u32[]{:S(2)}) copy-start(f32[896,128]{0,1:T(8,128)} %copy.118) | copy-start | bytes 1376260
  823.9 0.8 copy-start.7
  835.6 9.9 copy-start.8
  843.6 1.9 copy-start
  892.1 10.5 %copy-start.1 = (f32[1024,1024]{1,0:T(8,128)S(1)}, f32[1024,1024]{1,0:T(8,128)}, u32[]{:S(2)}) copy-start(f32[1024,1024]{1,0:T(8,128)} %copy-done) | copy-start | bytes 12582916
  911.3 0.7 copy-start.9
  949.2 10.5 %copy-start.2 = (f32[1024,1024]{1,0:T(8,128)S(1)}, f32[1024,1024]{1,0:T(8,128)}, u32[]{:S(2)}) copy-start(f32[1024,1024]{1,0:T(8,128)} %copy-done) | copy-start | bytes 12582916
  971.3 13.6 %copy-start.10 = (f32[128,128]{0,1:T(8,128)S(1)}, f32[128,128]{0,1:T(8,128)}, u32[]{:S(2)}) copy-start(f32[128,128]{0,1:T(8,128)} %copy.183) | copy-start | bytes 196612
Sparse Core Ops, SparseCore 0:
  46.8 283.5 all-reduce.4
  333.9 114.5 all-gather.4
where the time goes:
time: 1040 us; the launch traced here: 1030 us
  other arithmetic  365 us (35%)
  waiting for transfers between devices  311 us (30%)
  matrix products  166 us (16%)
  local copies, waits for them, and re-layouts  85.6 us (8%)
  blocking collectives  79.8 us (8%)
  between operations  23.2 us (2%)
    psum x1, waiting for transfers between devices, on_device(): total_zero, total_lag = lax.psum((gram_zero, gram_lag), ('traj', 'seg'))  198 us
    another operation x31, other arithmetic, subspace(): lower_factor = jnp.linalg.cholesky(c_zero)  168 us
    another operation x10, other arithmetic, tri_solve(): lax.linalg.triangular_solve(factor, rhs, left_side=True, lower=True, tran...  116 us
    all_gather x1, waiting for transfers between devices, on_device(): lax.all_gather(own_totals, ('traj', 'seg'), axis=0, tiled=True)  113 us
    another operation x108, matrix products, tri_solve(): lax.linalg.triangular_solve(factor, rhs, left_side=True, lower=True, tran...  97.6 us
    unnamed x1, blocking collectives  79.8 us
    another operation x9, other arithmetic, subspace(): small_factor = jnp.linalg.cholesky(gram_small)  37.6 us
    another operation x78, local copies, waits for them, and re-layouts, tri_solve(): lax.linalg.triangular_solve(factor, rhs, left_side=True, lower=True, tran...  34 us
  transfers between devices with their start and end apart: 3, of which 2 were waited for; matrix products, arithmetic and copies ran while one was open for 2% of the time, Pallas kernels for 0%

commit v1 on v0

v1 whole, which is shorter than its diff:
```python
import jax
import jax.numpy as jnp
from jax import lax
from jax.experimental import pallas as pl
from jax.experimental.pallas import tpu as pltpu
from jax.sharding import PartitionSpec as P

FEAT = 1024
K = 128
LAG = 10
ITERS = 3
TILE = 128
BLOCKS = FEAT // TILE
PANEL = 32

exact_mode = lax.Precision.HIGHEST
soft_square = 0.1
ridge_term = 0.01
spectral_shift = 2.0


def mm(a, b):
    return lax.dot_general(
        a, b, (((1,), (0,)), ((), ())), precision=exact_mode, preferred_element_type=jnp.float32
    )


def mm_t(a, b):
    return lax.dot_general(
        a, b, (((0,), (0,)), ((), ())), precision=exact_mode, preferred_element_type=jnp.float32
    )


def mm_nt(a, b):
    return lax.dot_general(
        a, b, (((1,), (1,)), ((), ())), precision=exact_mode, preferred_element_type=jnp.float32
    )


def inverse_factor(a):
    groups = [a[8 * g : 8 * g + 8, :] for g in range(16)]
    lane = lax.broadcasted_iota(jnp.int32, (8, TILE), 1)
    sub = lax.broadcasted_iota(jnp.int32, (8, TILE), 0)
    lane_one = lane[0:1, :]
    pivots = [jnp.ones((8, TILE), jnp.float32) for _ in range(16)]
    per = PANEL // 8
    for panel in range(TILE // PANEL):
        last = per * (panel + 1)
        for j in range(PANEL * panel, PANEL * (panel + 1)):
            home, at = j // 8, j % 8
            own = groups[home]
            column = jnp.broadcast_to(own[:, j : j + 1], (8, TILE))
            pivot = column[at : at + 1, :]
            inv = 1.0 / pivot
            scaled = jnp.where(lane_one == j, 1.0, own[at : at + 1, :]) * inv
            unit = jnp.where(sub == at, 1.0, 0.0)
            kept = jnp.where((lane == j) & (sub >= at), unit, own)
            groups[home] = kept - jnp.where(sub > at, column, 0.0) * scaled
            pivots[home] = jnp.where(sub == at, pivot, pivots[home])
            for g in range(home + 1, last):
                column = jnp.broadcast_to(groups[g][:, j : j + 1], (8, TILE))
                groups[g] = jnp.where(lane == j, 0.0, groups[g]) - column * scaled
        if last < 16:
            rows = jnp.concatenate(groups[last - per : last], axis=0)
            scale = jnp.concatenate(pivots[last - per : last], axis=0)
            here = lax.broadcasted_iota(jnp.int32, (PANEL, TILE), 0) + PANEL * panel
            across = lax.broadcasted_iota(jnp.int32, (PANEL, TILE), 1)
            done = (across > here) & (across < PANEL * (panel + 1))
            update = mm_t(rows, jnp.where(done, 0.0, rows / scale))
            inside = (lane >= PANEL * panel) & (lane < PANEL * (panel + 1))
            for g in range(last, 16):
                groups[g] = jnp.where(inside, 0.0, groups[g]) - update[8 * g : 8 * g + 8, :]
    out = []
    for g in range(16):
        root = lax.rsqrt(pivots[g])
        root = root * (1.5 - 0.5 * pivots[g] * root * root)
        out.append(jnp.where(lane <= sub + 8 * g, groups[g] * root, 0.0))
    return jnp.concatenate(out, axis=0)


def gram_body(x_ref, lag_ref, center_ref, valid_ref, paired_ref, stat_ref, out_ref):
    center = center_ref[0:1, :]
    valid = valid_ref[:, 0:1]
    paired = paired_ref[:, 0:1]
    base = x_ref[...] - center
    centered = base * valid
    lead = base * paired
    ahead = (lag_ref[...] - center) * paired
    left = jnp.concatenate([lead, ahead], axis=0)
    right = jnp.concatenate([ahead, lead], axis=0)
    sum_lead = jnp.sum(lead, axis=0, keepdims=True)
    sum_ahead = jnp.sum(ahead, axis=0, keepdims=True)
    row = lax.broadcasted_iota(jnp.int32, (8, FEAT), 0)
    stats = jnp.where(row == 1, sum_lead, jnp.where(row == 2, sum_ahead, stat_ref[...]))
    out_ref[:, 9, :, :] = jnp.zeros((BLOCKS, TILE, TILE), jnp.float32)
    for r in range(BLOCKS):
        lo = TILE * r
        upper = mm_t(centered[:, lo : lo + TILE], centered[:, lo:])
        for c in range(r, BLOCKS):
            out_ref[r, c, :, :] = upper[:, TILE * (c - r) : TILE * (c - r + 1)]
        lower = mm_t(left[:, lo : lo + TILE], right[:, : lo + TILE])
        for c in range(r):
            out_ref[r, c, :, :] = lower[:, TILE * c : TILE * (c + 1)]
        out_ref[r, 8, :, :] = lower[:, lo:]
        out_ref[r, 9, 0:8, :] = stats[:, lo : lo + TILE]


def solve_body(g_ref, x_ref, valid_ref, out_ref, m_ref, lag_ref, row_ref):
    def stat(kind):
        lo = 9 * TILE + 32 * kind
        return jnp.concatenate([g_ref[r, lo : lo + 32, :] for r in range(BLOCKS)], axis=1)

    sums, a_sum, b_sum, count, pair = stat(0), stat(1), stat(2), stat(3), stat(4)
    frames_total = jnp.sum(count, axis=0, keepdims=True)
    pairs_total = jnp.sum(pair, axis=0, keepdims=True)
    mean_all = jnp.sum(sums, axis=0, keepdims=True) / frames_total
    inv_pair = 1.0 / jnp.maximum(pair, 1.0)
    dev = sums / count - mean_all
    dev_a = dev + a_sum * inv_pair
    dev_b = dev + b_sum * inv_pair
    dev_a = dev_a - jnp.sum(pair * dev_a, axis=0, keepdims=True) / pairs_total
    dev_b = dev_b - jnp.sum(pair * dev_b, axis=0, keepdims=True) / pairs_total
    left_zero = dev * count
    left_lag = jnp.concatenate(
        [-a_sum * inv_pair, -b_sum * inv_pair, pair * dev_a, pair * dev_b], axis=0
    )
    right_lag = jnp.concatenate([b_sum, a_sum, dev_b, dev_a], axis=0)
    inv_frames = 1.0 / frames_total[:, :TILE]
    inv_pairs = 0.5 / pairs_total[:, :TILE]
    diagonal = lax.broadcasted_iota(jnp.int32, (TILE, TILE), 0) == lax.broadcasted_iota(
        jnp.int32, (TILE, TILE), 1
    )
    for r in range(BLOCKS):
        lo = TILE * r
        fix = mm_t(left_zero[:, lo : lo + TILE], dev[:, lo:])
        fix_lag = mm_t(left_lag[:, lo : lo + TILE], right_lag[:, : lo + TILE])
        for c in range(BLOCKS):
            at = TILE * c
            if c >= r:
                block = (g_ref[r, at : at + TILE, :] + fix[:, at - lo : at - lo + TILE]) * inv_frames
                if c == r:
                    block = jnp.where(diagonal, block + ridge_term, block)
                m_ref[lo : lo + TILE, at : at + TILE] = block
            else:
                m_ref[lo : lo + TILE, at : at + TILE] = jnp.zeros((TILE, TILE), jnp.float32)
            if c <= r:
                slot = 8 if c == r else c
                block = g_ref[r, TILE * slot : TILE * slot + TILE, :] + fix_lag[:, at : at + TILE]
                block = block * inv_pairs
                lag_ref[lo : lo + TILE, at : at + TILE] = block
                if c < r:
                    lag_ref[at : at + TILE, lo : lo + TILE] = block.T

    lane_all = lax.broadcasted_iota(jnp.int32, (TILE, FEAT), 1)

    def eliminate(k, carry):
        lo = pl.multiple_of(k * TILE, TILE)
        factor = inverse_factor(m_ref[pl.ds(lo, TILE), pl.ds(lo, TILE)])
        row_ref[...] = mm(factor, m_ref[pl.ds(lo, TILE), :])
        row_ref[:, pl.ds(lo, TILE)] = factor
        m_ref[pl.ds(lo, TILE), :] = row_ref[...]
        inside = (lane_all >= lo) & (lane_all < lo + TILE)

        def below(i, inner):
            at = pl.multiple_of(i * TILE, TILE)
            update = mm_t(row_ref[:, pl.ds(at, TILE)], row_ref[...])
            old = jnp.where(inside, 0.0, m_ref[pl.ds(at, TILE), :])
            m_ref[pl.ds(at, TILE), :] = old - update
            return inner

        return lax.fori_loop(k + 1, BLOCKS, below, carry)

    lax.fori_loop(0, BLOCKS, eliminate, 0)

    def solve_rows(q):
        return jnp.concatenate(
            [
                mm(m_ref[TILE * r : TILE * (r + 1), : TILE * (r + 1)], q[: TILE * (r + 1)])
                for r in range(BLOCKS)
            ],
            axis=0,
        )

    def solve_columns(q):
        return jnp.concatenate(
            [
                mm_t(m_ref[TILE * r :, TILE * r : TILE * (r + 1)], q[TILE * r :])
                for r in range(BLOCKS)
            ],
            axis=0,
        )

    def sweep(step, q):
        inner = solve_columns(q)
        return solve_rows(mm(lag_ref[...], inner)) + spectral_shift * q

    start = (
        lax.broadcasted_iota(jnp.int32, (FEAT, K), 0) == lax.broadcasted_iota(jnp.int32, (FEAT, K), 1)
    ).astype(jnp.float32)
    image = lax.fori_loop(0, ITERS, sweep, start)
    small = inverse_factor(mm_t(image, image))
    basis = mm_nt(solve_columns(image), small)
    shifted = (x_ref[...] - mean_all) * valid_ref[:, 0:1]
    out_ref[...] = mm(shifted, basis)


def gram_call(*args):
    return pl.pallas_call(
        gram_body,
        out_shape=jax.ShapeDtypeStruct((BLOCKS, 10, TILE, TILE), jnp.float32),
        compiler_params=pltpu.CompilerParams(vmem_limit_bytes=48 << 20),
        name="packed_scatter",
    )(*args)


def solve_call(*args):
    return pl.pallas_call(
        solve_body,
        out_shape=jax.ShapeDtypeStruct((TILE, K), jnp.float32),
        scratch_shapes=[
            pltpu.VMEM((FEAT, FEAT), jnp.float32),
            pltpu.VMEM((FEAT, FEAT), jnp.float32),
            pltpu.VMEM((TILE, FEAT), jnp.float32),
        ],
        compiler_params=pltpu.CompilerParams(vmem_limit_bytes=56 << 20),
        name="subspace",
    )(*args)


def featurize(frames, pairs):
    atoms = frames.shape[2]
    atom = lax.broadcasted_iota(jnp.int32, (atoms, FEAT), 0)
    pick = (atom == pairs[0:1]).astype(jnp.float32) - (atom == pairs[1:2]).astype(jnp.float32)
    offset = jnp.einsum(
        "tca,af->ctf", frames, pick, precision=exact_mode, preferred_element_type=jnp.float32
    )
    return jnp.sqrt(jnp.sum(offset * offset, axis=0) + soft_square)


def everywhere(x, axis, peers):
    return lax.all_to_all(jnp.broadcast_to(x[None], (peers,) + x.shape), axis, 0, 0)


def on_device(coords, pairs, lengths):
    segs = lax.axis_size("seg")
    trajs = lax.axis_size("traj")
    frames = coords[0]
    rows = frames.shape[0]
    features = featurize(frames, pairs)
    arriving = lax.ppermute(features[:LAG], "seg", [(i + 1, i) for i in range(segs - 1)])
    lagged = jnp.concatenate([features[LAG:], arriving], axis=0)
    index = lax.axis_index("seg") * rows + lax.broadcasted_iota(jnp.int32, (rows, TILE), 0)
    length = lengths[0]
    valid = (index < length).astype(jnp.float32)
    paired = (index + LAG < length).astype(jnp.float32)
    count = jnp.sum(valid[:, 0])
    pair_count = jnp.sum(paired[:, 0])
    sum_all = jnp.sum(features * valid[:, 0:1], axis=0)
    row = lax.broadcasted_iota(jnp.int32, (8, FEAT), 0)
    stat_rows = jnp.where(
        row == 0,
        sum_all,
        jnp.where(row == 3, count, jnp.where(row == 4, pair_count, 0.0)),
    )
    group = jnp.sum(everywhere(stat_rows, "seg", segs), axis=0)
    center = jnp.broadcast_to(group[0:1] / group[3:4], (8, FEAT))
    packed = gram_call(features, lagged, center, valid, paired, stat_rows)
    chunk = lax.psum_scatter(
        packed.reshape(BLOCKS * 10 * TILE, TILE), "seg", scatter_dimension=0, tiled=True
    )
    stats = chunk[9 * TILE : 9 * TILE + 8]
    sent = jnp.concatenate(
        [chunk.reshape(trajs, 40, TILE), jnp.broadcast_to(stats[None], (trajs, 8, TILE))], axis=1
    )
    taken = lax.all_to_all(sent, "traj", 0, 0)
    own = jnp.sum(taken[:, :40], axis=0)
    whole = everywhere(own, "traj", trajs).reshape(10 * TILE, TILE)[: 9 * TILE]
    group_stats = taken[:, 40:].transpose(1, 0, 2).reshape(8 * trajs, TILE)
    gathered = lax.all_gather(jnp.concatenate([whole, group_stats], axis=0), "seg", axis=0)
    projected = solve_call(gathered, features, valid)
    return projected[None]


def solution(mesh):
    return jax.shard_map(
        on_device,
        mesh=mesh,
        in_specs=(P("traj", "seg", None, None), P(), P("traj")),
        out_specs=P("traj", "seg", None),
        check_vma=False,
    )
```

time: 1040 us -> 351 us (0.34)
  other arithmetic: 365 us -> 4.6 us
  waiting for transfers between devices: 311 us -> 101 us
  Pallas kernels: 0 us -> 174 us
  matrix products: 166 us -> 3.82 us
  local copies, waits for them, and re-layouts: 85.6 us -> 3.57 us
  blocking collectives: 79.8 us -> 31.8 us
  starting transfers between devices: 2.22 us -> 14.5 us
    another operation x50 -> x0, other arithmetic: 322 us -> none  [the longest x31 168 us: subspace(): lower_factor = jnp.linalg.cholesky(c_zero)]
    psum x1 -> x0, waiting for transfers between devices: 198 us -> none  [on_device(): total_zero, total_lag = lax.psum((gram_zero, gram_lag), ('traj', 'seg'))]
    pallas_call x0 -> x2, Pallas kernels: none -> 174 us  [the longest x1 167 us: solve_call(): pl.pallas_call(solve_body, out_shape=jax.ShapeDtypeStruct((TILE, K), jnp....]
    another operation x122 -> x0, matrix products: 126 us -> none  [the longest x108 97.6 us: tri_solve(): lax.linalg.triangular_solve(factor, rhs, left_side=True, lower=True, tran...]
    unnamed x1 -> x0, blocking collectives: 79.8 us -> none
    all_gather x1, waiting for transfers between devices: 113 us -> 36.1 us  [on_device(): lax.all_gather(jnp.concatenate([whole, group_stats], axis=0), 'seg', axis=0)]
    another operation x103 -> x0, local copies, waits for them, and re-layouts: 43.8 us -> none  [the longest x78 34 us: tri_solve(): lax.linalg.triangular_solve(factor, rhs, left_side=True, lower=True, tran...]
    reduce_scatter x0 -> x1, waiting for transfers between devices: none -> 41.4 us  [on_device(): lax.psum_scatter(packed.reshape(BLOCKS * 10 * TILE, TILE), 'seg', scatter...]
  transfers between devices with their start and end apart: 3 -> 5, of which waited for: 2 -> 5; matrix products, arithmetic and copies ran while one was open for 2% -> 0% of each run, Pallas kernels for 0% -> 0%
where the time goes in v1:
time: 351 us; the launch traced here: 347 us
  Pallas kernels  174 us (50%)
  waiting for transfers between devices  101 us (29%)
  blocking collectives  31.8 us (9%)
  starting transfers between devices  14.5 us (4%)
  between operations  14.3 us (4%)
  other arithmetic  4.6 us (1%)
  matrix products  3.82 us (1%)
  local copies, waits for them, and re-layouts  3.57 us (1%)
    pallas_call x1, Pallas kernels, solve_call(): pl.pallas_call(solve_body, out_shape=jax.ShapeDtypeStruct((TILE, K), jnp....  167 us
    reduce_scatter x1, waiting for transfers between devices, on_device(): lax.psum_scatter(packed.reshape(BLOCKS * 10 * TILE, TILE), 'seg', scatter...  41.4 us
    all_gather x1, waiting for transfers between devices, on_device(): lax.all_gather(jnp.concatenate([whole, group_stats], axis=0), 'seg', axis=0)  36.1 us
    all_to_all x1, blocking collectives, on_device(): taken = lax.all_to_all(sent, 'traj', 0, 0)  31.8 us
    all_to_all x2, waiting for transfers between devices, everywhere(): lax.all_to_all(jnp.broadcast_to(x[None], (peers,) + x.shape), axis, 0, 0)  21.4 us
    all_to_all x2, starting transfers between devices, everywhere(): lax.all_to_all(jnp.broadcast_to(x[None], (peers,) + x.shape), axis, 0, 0)  11.8 us
  transfers between devices with their start and end apart: 5, of which 5 were waited for; matrix products, arithmetic and copies ran while one was open for 0% of the time, Pallas kernels for 0%

profile of v1, /device:TPU:6, one launch (start us, length us, event | category | flops | bytes accessed | tf_op | source)
XLA Modules:
  0.0 347.0 jit_solution(1447754401930407427)
XLA Ops:
  6.5 0.0 copy-start
  7.3 0.7 fusion.14
  7.9 0.6 compare_select_fusion
  8.5 0.8 fusion.16
  9.3 0.0 copy-done
  9.3 3.8 %fusion.8 = f32[1024,128]{1,0:T(8,128)S(1)} fusion(s32[1024]{0:T(1024)S(1)} %bitcast.34, s32[1024]{0:T(1024)S(1)} %bitcast.33, f32[1,128,3,512]{3,1,2,0:T(8,128)S(1)} %copy-done), kind=kOutput, calls=%fused_computation.8 | convolution fusion | flops 2419195904 | bytes 1318912 | tf_op jit(solution)/shard_map/tca,af->ctf/dot_general | solution.py:234
  13.1 0.2 copy.8
  13.3 0.3 multiply_reduce_fusion
  13.6 0.8 select_select_fusion.stat_ref
  14.4 0.7 broadcast_in_dim.48
  15.1 5.5 %all-to-all-start = ((f32[8,8,1024]{2,1,0:T(8,128)}), f32[8,8,1024]{2,1,0:T(8,128)S(1)}, u32[]{:S(2)}, u32[]{:S(2)}) async-start(f32[8,8,1024]{2,1,0:T(8,128)} %broadcast_in_dim.48), calls=%async_computation | async-start | bytes 524288 | tf_op jit(solution)/shard_map/all_to_all | solution.py:241
  20.6 0.0 reduce-scatter.2.cloned.1.call-start
  20.6 0.1 sqrt_bitcast_fusion.x_ref
  20.8 0.0 copy-start.1
  20.8 2.5 collective-permute-start
  23.3 1.8 collective-permute-done
  25.2 0.8 all-to-all-done
  26.1 0.1 iota.39.paired_ref
  26.2 0.1 iota.38.valid_ref
  26.2 0.0 copy-start.2
  26.3 6.7 %packed_scatter.1 = f32[8,10,128,128]{3,2,1,0:T(8,128)} custom-call(f32[128,1024]{1,0:T(8,128)S(1)} %sqrt_bitcast_fusion.x_ref, f32[128,1024]{1,0:T(8,128)S(1)} %pad_maximum_fusion.2.lag_ref, f32[8,1024]{1,0:T(8,128)S(1)} %broadcast_in_dim.50.center_ref, f32[128,128]{1,0:T(8,128)S(1)} %iota.38.valid_ref, f32[128,128]{1,0:T(8,128)S(1)} %iota.39.paired_ref, ...), custom_call_target="tpu_custom_call" | custom-call | tf_op jit(solution)/shard_map/packed_scatter/pallas_call | solution.py:208
  32.9 0.0 copy-done.1
  32.9 0.0 copy-done.2
  32.9 0.0 reduce-scatter.2.cloned.1.call-update
  33.0 41.4 %reduce-scatter.2.cloned.1.call-done = f32[1280,128]{1,0:T(8,128)} async-done(((f32[10240,128]{1,0:T(8,128)}), f32[1280,128]{1,0:T(8,128)}) %reduce-scatter.2.cloned.1.call-update) | async-done | bytes 655376 | tf_op jit(solution)/shard_map/reduce_scatter | solution.py:268
  74.3 0.7 slice.47
  75.0 1.2 pad_maximum_fusion
  76.2 31.8 %all_to_all.15 = f32[32,48,128]{2,1,0:T(8,128)S(1)} all-to-all(f32[32,48,128]{2,1,0:T(8,128)S(1)} %pad_maximum_fusion), channel_id=1, replica_groups=mesh['traj'=32,'seg'=8] {'traj'}, dimensions={0} | all-to-all | bytes 1572864 | tf_op jit(solution)/shard_map/all_to_all | solution.py:275
  108.0 0.1 slice_reduce_fusion
  108.0 0.9 broadcast_in_dim.52
  108.9 6.2 %all-to-all-start.2 = ((f32[32,40,128]{2,1,0:T(8,128)}), f32[32,40,128]{2,1,0:T(8,128)S(1)}, u32[]{:S(2)}, u32[]{:S(2)}) async-start(f32[32,40,128]{2,1,0:T(8,128)} %broadcast_in_dim.52), calls=%async_computation.3 | async-start | bytes 1310720 | tf_op jit(solution)/shard_map/all_to_all | solution.py:241
  115.1 0.2 all-gather.3.cloned.1.call-start
  115.4 20.6 %all-to-all-done.2 = f32[32,40,128]{2,1,0:T(8,128)S(1)} async-done(((f32[32,40,128]{2,1,0:T(8,128)}), f32[32,40,128]{2,1,0:T(8,128)S(1)}, u32[]{:S(2)}, u32[]{:S(2)}) %all-to-all-start.2) | async-done | bytes 655392 | tf_op jit(solution)/shard_map/all_to_all | solution.py:241
  136.1 0.9 pad_maximum_fusion.1
  137.0 0.0 all-gather.3.cloned.1.call-update
  137.0 36.1 %all-gather.3.cloned.1.call-done = f32[11264,128]{1,0:T(8,128)} async-done(((f32[1408,128]{1,0:T(8,128)}), f32[11264,128]{1,0:T(8,128)}) %all-gather.3.cloned.1.call-update) | async-done | bytes 5767184 | tf_op jit(solution)/shard_map/all_gather | solution.py:279
  173.1 167.1 %subspace.1 = f32[128,128]{1,0:T(8,128)} custom-call(f32[8,1408,128]{2,1,0:T(8,128)} %bitcast.28, f32[128,1024]{1,0:T(8,128)} %copy-done.1, f32[128,128]{1,0:T(8,128)} %copy-done.2), custom_call_target="tpu_custom_call" | custom-call | tf_op jit(solution)/shard_map/subspace/pallas_call | solution.py:217
  (11 shorter events, 0.2 us)
Async XLA Ops:
  6.5 2.8 copy-start
  15.1 11.0 %all-to-all-start = ((f32[8,8,1024]{2,1,0:T(8,128)}), f32[8,8,1024]{2,1,0:T(8,128)S(1)}, u32[]{:S(2)}, u32[]{:S(2)}) async-start(f32[8,8,1024]{2,1,0:T(8,128)} %broadcast_in_dim.48), calls=%async_computation | async-start | bytes 524288 | tf_op jit(solution)/shard_map/all_to_all | solution.py:241
  20.6 53.7 %reduce-scatter.2.cloned.1.call-start = ((), (), s32[]{:S(2)}) async-start(), calls=%async_computation.4 | async-start | bytes 5898240 | tf_op jit(solution)/shard_map/reduce_scatter | solution.py:268
  20.8 12.2 %copy-start.1 = (f32[128,1024]{1,0:T(8,128)}, f32[128,1024]{1,0:T(8,128)S(1)}, u32[]{:S(2)}) copy-start(f32[128,1024]{1,0:T(8,128)S(1)} %sqrt_bitcast_fusion.x_ref) | copy-start | bytes 1572868
  20.8 4.4 %collective-permute-start = (f32[10,1024]{1,0:T(8,128)S(1)}, f32[10,1024]{1,0:T(8,128)S(1)}, u32[]{:S(2)}, u32[]{:S(2)}) collective-permute-start(f32[10,1024]{1,0:T(8,128)S(1)} %slice.44), channel_id=1, source_target_pairs={{1,0},{2,1},{3,2},{4,3},{5,4},{6,5},{7,6},{9,8},{10,9},{11,10},{12... | collective-permute-start | bytes 122888 | tf_op jit(solution)/shard_map/ppermute | solution.py:250
  26.2 6.7 %copy-start.2 = (f32[128,128]{1,0:T(8,128)}, f32[128,128]{1,0:T(8,128)S(1)}, u32[]{:S(2)}) copy-start(f32[128,128]{1,0:T(8,128)S(1)} %iota.38.valid_ref) | copy-start | bytes 196612
  108.9 27.1 %all-to-all-start.2 = ((f32[32,40,128]{2,1,0:T(8,128)}), f32[32,40,128]{2,1,0:T(8,128)S(1)}, u32[]{:S(2)}, u32[]{:S(2)}) async-start(f32[32,40,128]{2,1,0:T(8,128)} %broadcast_in_dim.52), calls=%async_computation.3 | async-start | bytes 1310720 | tf_op jit(solution)/shard_map/all_to_all | solution.py:241
  115.1 57.9 %all-gather.3.cloned.1.call-start = ((), (), s32[]{:S(2)}) async-start(), calls=%async_computation.5 | async-start | bytes 6488064 | tf_op jit(solution)/shard_map/all_gather | solution.py:279
Sparse Core Ops, SparseCore 0:
  33.1 41.2 reduce-scatter.1
  137.1 35.9 all-gather.2

commit v2 on v1

--- a/solution.py
+++ b/solution.py
@@ -46,20 +46,34 @@
     per = PANEL // 8
     for panel in range(TILE // PANEL):
         last = per * (panel + 1)
-        for j in range(PANEL * panel, PANEL * (panel + 1)):
-            home, at = j // 8, j % 8
-            own = groups[home]
-            column = jnp.broadcast_to(own[:, j : j + 1], (8, TILE))
-            pivot = column[at : at + 1, :]
-            inv = 1.0 / pivot
-            scaled = jnp.where(lane_one == j, 1.0, own[at : at + 1, :]) * inv
-            unit = jnp.where(sub == at, 1.0, 0.0)
-            kept = jnp.where((lane == j) & (sub >= at), unit, own)
-            groups[home] = kept - jnp.where(sub > at, column, 0.0) * scaled
-            pivots[home] = jnp.where(sub == at, pivot, pivots[home])
-            for g in range(home + 1, last):
-                column = jnp.broadcast_to(groups[g][:, j : j + 1], (8, TILE))
-                groups[g] = jnp.where(lane == j, 0.0, groups[g]) - column * scaled
+        for home in range(last - per, last):
+            base = 8 * home
+            columns = [
+                [jnp.broadcast_to(groups[g][:, base + q : base + q + 1], (8, TILE)) for q in range(8)]
+                for g in range(home, last)
+            ]
+            for j in range(8):
+                pivot = jnp.broadcast_to(columns[0][j][j : j + 1, :], (8, TILE))
+                inv = 1.0 / pivot
+                here = lane == base + j
+                own = jnp.broadcast_to(groups[home][j : j + 1, :], (8, TILE))
+                scaled = jnp.where(here, 1.0, own) * inv
+                factors = [
+                    jnp.broadcast_to(columns[0][q][j : j + 1, :], (8, TILE)) * inv
+                    for q in range(j + 1, 8)
+                ]
+                pivots[home] = jnp.where(sub == j, pivot, pivots[home])
+                for g in range(home, last):
+                    column = columns[g - home][j]
+                    if g == home:
+                        unit = jnp.where(sub == j, 1.0, 0.0)
+                        column = jnp.where(sub > j, column, 0.0)
+                        kept = jnp.where(here & (sub >= j), unit, groups[g])
+                    else:
+                        kept = jnp.where(here, 0.0, groups[g])
+                    groups[g] = kept - column * scaled
+                    for q in range(j + 1, 8):
+                        columns[g - home][q] = columns[g - home][q] - column * factors[q - j - 1]
         if last < 16:
             rows = jnp.concatenate(groups[last - per : last], axis=0)
             scale = jnp.concatenate(pivots[last - per : last], axis=0)
@@ -197,7 +211,9 @@
     start = (
         lax.broadcasted_iota(jnp.int32, (FEAT, K), 0) == lax.broadcasted_iota(jnp.int32, (FEAT, K), 1)
     ).astype(jnp.float32)
-    image = lax.fori_loop(0, ITERS, sweep, start)
+    first = mm_nt(lag_ref[:, :TILE], m_ref[:TILE, :TILE])
+    image = solve_rows(first) + spectral_shift * start
+    image = lax.fori_loop(1, ITERS, sweep, image)
     small = inverse_factor(mm_t(image, image))
     basis = mm_nt(solve_columns(image), small)
     shifted = (x_ref[...] - mean_all) * valid_ref[:, 0:1]

time: 351 us -> 277 us (0.79)
  Pallas kernels: 174 us -> 100 us
    pallas_call x1, Pallas kernels: 167 us -> 93.8 us  [solve_call(): pl.pallas_call(solve_body, out_shape=jax.ShapeDtypeStruct((TILE, K), jnp....]
where the time goes in v2:
time: 277 us; the launch traced here: 274 us
  waiting for transfers between devices  101 us (36%)
  Pallas kernels  100 us (36%)
  blocking collectives  31.8 us (11%)
  starting transfers between devices  14.5 us (5%)
  between operations  14.3 us (5%)
  other arithmetic  4.6 us (2%)
  matrix products  3.82 us (1%)
  local copies, waits for them, and re-layouts  3.57 us (1%)
    pallas_call x1, Pallas kernels, solve_call(): pl.pallas_call(solve_body, out_shape=jax.ShapeDtypeStruct((TILE, K), jnp....  93.8 us
    reduce_scatter x1, waiting for transfers between devices, on_device(): lax.psum_scatter(packed.reshape(BLOCKS * 10 * TILE, TILE), 'seg', scatter...  41.4 us
    all_gather x1, waiting for transfers between devices, on_device(): lax.all_gather(jnp.concatenate([whole, group_stats], axis=0), 'seg', axis=0)  36.1 us
    all_to_all x1, blocking collectives, on_device(): taken = lax.all_to_all(sent, 'traj', 0, 0)  31.8 us
    all_to_all x2, waiting for transfers between devices, everywhere(): lax.all_to_all(jnp.broadcast_to(x[None], (peers,) + x.shape), axis, 0, 0)  21.4 us
    all_to_all x2, starting transfers between devices, everywhere(): lax.all_to_all(jnp.broadcast_to(x[None], (peers,) + x.shape), axis, 0, 0)  11.8 us
    pallas_call x1, Pallas kernels, gram_call(): pl.pallas_call(gram_body, out_shape=jax.ShapeDtypeStruct((BLOCKS, 10, TIL...  6.67 us
  transfers between devices with their start and end apart: 5, of which 5 were waited for; matrix products, arithmetic and copies ran while one was open for 0% of the time, Pallas kernels for 0%

profile of v2, /device:TPU:6, one launch (start us, length us, event | category | flops | bytes accessed | tf_op | source)
XLA Modules:
  0.0 273.7 jit_solution(11168303633797102041)
XLA Ops:
  6.5 0.0 copy-start
  7.3 0.7 fusion.14
  7.9 0.6 compare_select_fusion
  8.5 0.8 fusion.16
  9.3 0.0 copy-done
  9.3 3.8 %fusion.8 = f32[1024,128]{1,0:T(8,128)S(1)} fusion(s32[1024]{0:T(1024)S(1)} %bitcast.34, s32[1024]{0:T(1024)S(1)} %bitcast.33, f32[1,128,3,512]{3,1,2,0:T(8,128)S(1)} %copy-done), kind=kOutput, calls=%fused_computation.8 | convolution fusion | flops 2419195904 | bytes 1318912 | tf_op jit(solution)/shard_map/tca,af->ctf/dot_general | solution.py:250
  13.1 0.2 copy.8
  13.3 0.3 multiply_reduce_fusion
  13.6 0.8 select_select_fusion.stat_ref
  14.4 0.7 broadcast_in_dim.48
  15.1 5.5 %all-to-all-start = ((f32[8,8,1024]{2,1,0:T(8,128)}), f32[8,8,1024]{2,1,0:T(8,128)S(1)}, u32[]{:S(2)}, u32[]{:S(2)}) async-start(f32[8,8,1024]{2,1,0:T(8,128)} %broadcast_in_dim.48), calls=%async_computation | async-start | bytes 524288 | tf_op jit(solution)/shard_map/all_to_all | solution.py:257
  20.6 0.0 reduce-scatter.2.cloned.1.call-start
  20.6 0.1 sqrt_bitcast_fusion.x_ref
  20.8 0.0 copy-start.1
  20.8 2.5 collective-permute-start
  23.3 1.8 collective-permute-done
  25.2 0.8 all-to-all-done
  26.1 0.1 iota.39.paired_ref
  26.2 0.1 iota.38.valid_ref
  26.2 0.0 copy-start.2
  26.3 6.7 %packed_scatter.1 = f32[8,10,128,128]{3,2,1,0:T(8,128)} custom-call(f32[128,1024]{1,0:T(8,128)S(1)} %sqrt_bitcast_fusion.x_ref, f32[128,1024]{1,0:T(8,128)S(1)} %pad_maximum_fusion.2.lag_ref, f32[8,1024]{1,0:T(8,128)S(1)} %broadcast_in_dim.50.center_ref, f32[128,128]{1,0:T(8,128)S(1)} %iota.38.valid_ref, f32[128,128]{1,0:T(8,128)S(1)} %iota.39.paired_ref, ...), custom_call_target="tpu_custom_call" | custom-call | tf_op jit(solution)/shard_map/packed_scatter/pallas_call | solution.py:224
  32.9 0.0 copy-done.1
  32.9 0.0 copy-done.2
  32.9 0.0 reduce-scatter.2.cloned.1.call-update
  33.0 41.4 %reduce-scatter.2.cloned.1.call-done = f32[1280,128]{1,0:T(8,128)} async-done(((f32[10240,128]{1,0:T(8,128)}), f32[1280,128]{1,0:T(8,128)}) %reduce-scatter.2.cloned.1.call-update) | async-done | bytes 655376 | tf_op jit(solution)/shard_map/reduce_scatter | solution.py:284
  74.3 0.7 slice.47
  75.0 1.2 pad_maximum_fusion
  76.2 31.8 %all_to_all.15 = f32[32,48,128]{2,1,0:T(8,128)S(1)} all-to-all(f32[32,48,128]{2,1,0:T(8,128)S(1)} %pad_maximum_fusion), channel_id=1, replica_groups=mesh['traj'=32,'seg'=8] {'traj'}, dimensions={0} | all-to-all | bytes 1572864 | tf_op jit(solution)/shard_map/all_to_all | solution.py:291
  108.0 0.1 slice_reduce_fusion
  108.0 0.9 broadcast_in_dim.52
  108.9 6.2 %all-to-all-start.2 = ((f32[32,40,128]{2,1,0:T(8,128)}), f32[32,40,128]{2,1,0:T(8,128)S(1)}, u32[]{:S(2)}, u32[]{:S(2)}) async-start(f32[32,40,128]{2,1,0:T(8,128)} %broadcast_in_dim.52), calls=%async_computation.3 | async-start | bytes 1310720 | tf_op jit(solution)/shard_map/all_to_all | solution.py:257
  115.1 0.2 all-gather.3.cloned.1.call-start
  115.4 20.6 %all-to-all-done.2 = f32[32,40,128]{2,1,0:T(8,128)S(1)} async-done(((f32[32,40,128]{2,1,0:T(8,128)}), f32[32,40,128]{2,1,0:T(8,128)S(1)}, u32[]{:S(2)}, u32[]{:S(2)}) %all-to-all-start.2) | async-done | bytes 655392 | tf_op jit(solution)/shard_map/all_to_all | solution.py:257
  136.1 0.9 pad_maximum_fusion.1
  137.0 0.0 all-gather.3.cloned.1.call-update
  137.0 36.1 %all-gather.3.cloned.1.call-done = f32[11264,128]{1,0:T(8,128)} async-done(((f32[1408,128]{1,0:T(8,128)}), f32[11264,128]{1,0:T(8,128)}) %all-gather.3.cloned.1.call-update) | async-done | bytes 5767184 | tf_op jit(solution)/shard_map/all_gather | solution.py:295
  173.1 93.8 %subspace.1 = f32[128,128]{1,0:T(8,128)} custom-call(f32[8,1408,128]{2,1,0:T(8,128)} %bitcast.28, f32[128,1024]{1,0:T(8,128)} %copy-done.1, f32[128,128]{1,0:T(8,128)} %copy-done.2), custom_call_target="tpu_custom_call" | custom-call | tf_op jit(solution)/shard_map/subspace/pallas_call | solution.py:233
  (11 shorter events, 0.2 us)
Async XLA Ops:
  6.5 2.8 %copy-start = (f32[1,128,3,512]{3,1,2,0:T(8,128)S(1)}, f32[1,128,3,512]{3,1,2,0:T(8,128)}, u32[]{:S(2)}) copy-start(f32[1,128,3,512]{3,1,2,0:T(8,128)} %param.3) | copy-start | bytes 2359300
  15.1 11.0 %all-to-all-start = ((f32[8,8,1024]{2,1,0:T(8,128)}), f32[8,8,1024]{2,1,0:T(8,128)S(1)}, u32[]{:S(2)}, u32[]{:S(2)}) async-start(f32[8,8,1024]{2,1,0:T(8,128)} %broadcast_in_dim.48), calls=%async_computation | async-start | bytes 524288 | tf_op jit(solution)/shard_map/all_to_all | solution.py:257
  20.6 53.7 %reduce-scatter.2.cloned.1.call-start = ((), (), s32[]{:S(2)}) async-start(), calls=%async_computation.4 | async-start | bytes 5898240 | tf_op jit(solution)/shard_map/reduce_scatter | solution.py:284
  20.8 12.2 %copy-start.1 = (f32[128,1024]{1,0:T(8,128)}, f32[128,1024]{1,0:T(8,128)S(1)}, u32[]{:S(2)}) copy-start(f32[128,1024]{1,0:T(8,128)S(1)} %sqrt_bitcast_fusion.x_ref) | copy-start | bytes 1572868
  20.8 4.4 %collective-permute-start = (f32[10,1024]{1,0:T(8,128)S(1)}, f32[10,1024]{1,0:T(8,128)S(1)}, u32[]{:S(2)}, u32[]{:S(2)}) collective-permute-start(f32[10,1024]{1,0:T(8,128)S(1)} %slice.44), channel_id=1, source_target_pairs={{1,0},{2,1},{3,2},{4,3},{5,4},{6,5},{7,6},{9,8},{10,9},{11,10},{12... | collective-permute-start | bytes 122888 | tf_op jit(solution)/shard_map/ppermute | solution.py:266
  26.2 6.7 %copy-start.2 = (f32[128,128]{1,0:T(8,128)}, f32[128,128]{1,0:T(8,128)S(1)}, u32[]{:S(2)}) copy-start(f32[128,128]{1,0:T(8,128)S(1)} %iota.38.valid_ref) | copy-start | bytes 196612
  108.9 27.1 %all-to-all-start.2 = ((f32[32,40,128]{2,1,0:T(8,128)}), f32[32,40,128]{2,1,0:T(8,128)S(1)}, u32[]{:S(2)}, u32[]{:S(2)}) async-start(f32[32,40,128]{2,1,0:T(8,128)} %broadcast_in_dim.52), calls=%async_computation.3 | async-start | bytes 1310720 | tf_op jit(solution)/shard_map/all_to_all | solution.py:257
  115.1 57.9 %all-gather.3.cloned.1.call-start = ((), (), s32[]{:S(2)}) async-start(), calls=%async_computation.5 | async-start | bytes 6488064 | tf_op jit(solution)/shard_map/all_gather | solution.py:295
Sparse Core Ops, SparseCore 0:
  33.1 41.2 reduce-scatter.1
  137.1 35.9 all-gather.2
